TPU v7x, 512 devices: a whole 4x8x8 slice. The times are simulated.
512 devices in a mesh: fsdp: 32 (over z_lo, x, core), cp: 16 (over y, z_hi).
Axes of the slice: x: 4, y: 8, z: 8 (z_hi: 2, z_lo: 4; z = z_hi * 4 + z_lo), core: 2. Of those that a mesh axis runs over, the one named last changes fastest.
Arguments:
- queries: bfloat16 [4096, 16384], P('cp', 'fsdp'), may hold values from -8 to 8
- key_vectors: bfloat16 [4096, 1024], P(('fsdp', 'cp')), may hold values from -8 to 8
- value_vectors: bfloat16 [4096, 1024], P(('fsdp', 'cp')), may hold values from -6 to 6
- out_grads: bfloat16 [4096, 16384], P('cp', 'fsdp'), may hold values from -6 to 6
- pair_order: int32 [32], replicated, may hold values from 0 to 31, as said below
Outputs:
- attended: bfloat16 [4096, 16384], P('cp', 'fsdp')
- query_grads: bfloat16 [4096, 16384], P('cp', 'fsdp')
- key_grads: float32 [4096, 1024], P(('fsdp', 'cp'))
- value_grads: float32 [4096, 1024], P(('fsdp', 'cp'))
Inputs may be any that keep to these rules, and one draw needn't show every extreme that they name: `pair_order`: A permutation of the stretches; slots 2 c and 2 c + 1 hold stretches P and 31 - P for some P, in either order.
All inputs are finite; a program needn't handle non-finite values.
Results may differ from a plain program's by a relative error of at most 0.034.
Values may be sent and summed in bfloat16 or wider, within the bound.
No kernel may reach another device: no remote copies, remote signals or barrier semaphores. Data moves between devices by JAX's collectives and lax.ppermute only.
A program may use at most 64 MiB of HBM per device.

v0:
```python
import math
import jax
import jax.numpy as jnp
from jax import lax
from jax.sharding import PartitionSpec as P

HD = 128
NEG_FILL = -1e30


def block_scores(query_rows, key_part, positions, key_start, score_scale):
    scores = (
        jnp.einsum("nhd,jd->hnj", query_rows, key_part, preferred_element_type=jnp.float32)
        * score_scale
    )
    key_positions = key_start + jnp.arange(key_part.shape[0], dtype=jnp.int32)
    visible = key_positions[None, :] <= positions[:, None]
    return (scores, visible[None, :, :])


def attend(whole_k, whole_v, query_rows, positions, blocks, block_width):
    row_count, head_count, head_dim = query_rows.shape
    score_scale = 1.0 / math.sqrt(head_dim)

    def online_step(block_index, state_three):
        row_peak, row_total, value_sum = state_three
        key_start = block_index * block_width
        key_part = lax.dynamic_slice_in_dim(whole_k, key_start, block_width, 0)
        value_part = lax.dynamic_slice_in_dim(whole_v, key_start, block_width, 0)
        scores, visible = block_scores(query_rows, key_part, positions, key_start, score_scale)
        masked = jnp.where(visible, scores, NEG_FILL)
        new_peak = jnp.maximum(row_peak, jnp.max(masked, axis=2))
        factor = jnp.exp(row_peak - new_peak)
        weights = jnp.where(visible, jnp.exp(masked - new_peak[:, :, None]), 0.0)
        row_total = row_total * factor + jnp.sum(weights, axis=2)
        weight_half = weights.astype(jnp.bfloat16)
        block_sum = jnp.einsum(
            "hnj,jd->nhd", weight_half, value_part, preferred_element_type=jnp.float32
        )
        value_sum = value_sum * factor.T[:, :, None] + block_sum
        return (new_peak, row_total, value_sum)

    first_peak = jnp.full((head_count, row_count), NEG_FILL, jnp.float32)
    first_total = jnp.zeros((head_count, row_count), jnp.float32)
    first_sum = jnp.zeros((row_count, head_count, head_dim), jnp.float32)
    row_peak, row_total, value_sum = lax.fori_loop(
        0, blocks, online_step, (first_peak, first_total, first_sum)
    )
    log_total = row_peak + jnp.log(row_total)
    output = value_sum / row_total.T[:, :, None]
    return (output.astype(jnp.bfloat16), log_total)


def backprop(
    whole_k,
    whole_v,
    query_rows,
    grad_rows,
    positions,
    log_total,
    row_delta,
    blocks,
    block_width,
    key_acc,
    value_acc,
):
    row_count, head_count, head_dim = query_rows.shape
    score_scale = 1.0 / math.sqrt(head_dim)

    def grad_step(block_index, state_three):
        query_grad, key_sums, value_sums = state_three
        key_start = block_index * block_width
        key_part = lax.dynamic_slice_in_dim(whole_k, key_start, block_width, 0)
        value_part = lax.dynamic_slice_in_dim(whole_v, key_start, block_width, 0)
        scores, visible = block_scores(query_rows, key_part, positions, key_start, score_scale)
        prob_exact = jnp.where(visible, jnp.exp(scores - log_total[:, :, None]), 0.0)
        prob_half = prob_exact.astype(jnp.bfloat16)
        prob_grad = jnp.einsum(
            "nhd,jd->hnj", grad_rows, value_part, preferred_element_type=jnp.float32
        )
        score_grad = (prob_exact * (prob_grad - row_delta[:, :, None]) * score_scale).astype(
            jnp.bfloat16
        )
        query_grad = query_grad + jnp.einsum(
            "hnj,jd->nhd", score_grad, key_part, preferred_element_type=jnp.float32
        )
        key_term = jnp.einsum(
            "hnj,nhd->jd", score_grad, query_rows, preferred_element_type=jnp.float32
        )
        value_term = jnp.einsum(
            "hnj,nhd->jd", prob_half, grad_rows, preferred_element_type=jnp.float32
        )
        old_keys = lax.dynamic_slice_in_dim(key_sums, key_start, block_width, 0)
        old_values = lax.dynamic_slice_in_dim(value_sums, key_start, block_width, 0)
        key_sums = lax.dynamic_update_slice_in_dim(key_sums, old_keys + key_term, key_start, 0)
        value_sums = lax.dynamic_update_slice_in_dim(
            value_sums, old_values + value_term, key_start, 0
        )
        return (query_grad, key_sums, value_sums)

    first_grad = jnp.zeros((row_count, head_count, head_dim), jnp.float32)
    query_grad, key_acc, value_acc = lax.fori_loop(
        0, blocks, grad_step, (first_grad, key_acc, value_acc)
    )
    return (query_grad.astype(jnp.bfloat16), key_acc, value_acc)


def fetch_keys(key_vectors, value_vectors):
    fsdp_size = lax.axis_size("fsdp")
    kv_heads = key_vectors.shape[1] // HD
    repeats = fsdp_size // kv_heads
    rows_k, rows_v = (
        lax.all_gather(key_vectors, "cp", axis=0, tiled=True),
        lax.all_gather(value_vectors, "cp", axis=0, tiled=True),
    )
    gathered_rows = rows_k.shape[0]
    spread_k = jnp.repeat(rows_k.reshape(gathered_rows, kv_heads, HD), repeats, axis=1)
    spread_v = jnp.repeat(rows_v.reshape(gathered_rows, kv_heads, HD), repeats, axis=1)
    got_k, got_v = (
        lax.all_to_all(spread_k, "fsdp", split_axis=1, concat_axis=0, tiled=True),
        lax.all_to_all(spread_v, "fsdp", split_axis=1, concat_axis=0, tiled=True),
    )
    return (got_k.reshape(-1, HD), got_v.reshape(-1, HD))


def per_device(queries, key_vectors, value_vectors, out_grads, pair_order):
    tok_rows = queries.shape[0]
    q_heads = queries.shape[1] // HD
    kv_heads = key_vectors.shape[1] // HD
    half_rows = tok_rows // 2
    cp_size = lax.axis_size("cp")
    fsdp_size = lax.axis_size("fsdp")
    repeats = fsdp_size // kv_heads
    seq_len = tok_rows * cp_size
    block_width = math.gcd(256, seq_len)
    my_index = lax.axis_index("cp")
    first_stretch = pair_order[2 * my_index]
    second_stretch = pair_order[2 * my_index + 1]
    offsets = jnp.arange(tok_rows, dtype=jnp.int32)
    positions = jnp.where(
        offsets < half_rows,
        first_stretch * half_rows + offsets,
        second_stretch * half_rows + offsets - half_rows,
    )
    query_rows = queries.reshape(tok_rows, q_heads, HD)
    grad_rows = out_grads.reshape(tok_rows, q_heads, HD)
    whole_k, whole_v = fetch_keys(key_vectors, value_vectors)
    row_spans = ((0, tok_rows, jnp.maximum(first_stretch, second_stretch) + 1),)
    row_low, row_high, stretch_end = row_spans[0]
    blocks = (stretch_end * half_rows + block_width - 1) // block_width
    span_out, span_log = attend(whole_k, whole_v, query_rows, positions, blocks, block_width)
    row_delta = jnp.sum(grad_rows.astype(jnp.float32) * span_out.astype(jnp.float32), axis=2).T
    whole_k, whole_v = fetch_keys(key_vectors, value_vectors)
    key_acc = jnp.zeros((seq_len, HD), jnp.float32)
    value_acc = jnp.zeros((seq_len, HD), jnp.float32)
    span_grad, key_acc, value_acc = backprop(
        whole_k,
        whole_v,
        query_rows,
        grad_rows,
        positions,
        span_log,
        row_delta,
        blocks,
        block_width,
        key_acc,
        value_acc,
    )
    piece_rows = seq_len // fsdp_size
    term_k = key_acc.reshape(fsdp_size, piece_rows, HD)
    term_v = value_acc.reshape(fsdp_size, piece_rows, HD)
    got_k, got_v = (
        lax.all_to_all(
            term_k.astype(jnp.bfloat16), "fsdp", split_axis=0, concat_axis=0, tiled=True
        ).astype(term_k.dtype),
        lax.all_to_all(
            term_v.astype(jnp.bfloat16), "fsdp", split_axis=0, concat_axis=0, tiled=True
        ).astype(term_v.dtype),
    )
    summed_k = (
        got_k.reshape(kv_heads, repeats, piece_rows, HD)
        .sum(axis=1)
        .transpose(1, 0, 2)
        .reshape(piece_rows, kv_heads * HD)
    )
    summed_v = (
        got_v.reshape(kv_heads, repeats, piece_rows, HD)
        .sum(axis=1)
        .transpose(1, 0, 2)
        .reshape(piece_rows, kv_heads * HD)
    )
    final_k, final_v = (
        lax.psum_scatter(
            summed_k.astype(jnp.bfloat16), "cp", scatter_dimension=0, tiled=True
        ).astype(jnp.float32),
        lax.psum_scatter(
            summed_v.astype(jnp.bfloat16), "cp", scatter_dimension=0, tiled=True
        ).astype(jnp.float32),
    )
    attended = span_out.reshape(tok_rows, q_heads * HD)
    query_grads = span_grad.reshape(tok_rows, q_heads * HD)
    return (attended, query_grads, final_k, final_v)


def solution(mesh):
    return jax.shard_map(
        per_device,
        mesh=mesh,
        in_specs=(
            P("cp", "fsdp"),
            P(("fsdp", "cp"), None),
            P(("fsdp", "cp"), None),
            P("cp", "fsdp"),
            P(),
        ),
        out_specs=(
            P("cp", "fsdp"),
            P("cp", "fsdp"),
            P(("fsdp", "cp"), None),
            P(("fsdp", "cp"), None),
        ),
        check_vma=False,
    )
```

profile of v0, /device:TPU:4, one launch (start us, length us, event | category | flops | bytes accessed | tf_op | source)
XLA Modules:
  0.0 769.0 jit_solution(10527921880946531678)
XLA Ops:
  7.2 59.9 %all_gather.9 = bf16[128,1024]{1,0:T(8,128)(2,1)S(1)} all-gather(bf16[8,1024]{1,0:T(8,128)(2,1)} %param.11), channel_id=1, replica_groups=mesh['fsdp'=32,'cp'=16] {'cp'}, dimensions={0}, use_global_device_ids=true | all-gather | bytes 278528 | tf_op jit(solution)/shard_map/all_gather | solution.py:114
  67.1 1.2 broadcast_in_dim.54
  68.3 6.8 all-to-all-start.1
  75.2 62.8 %all_gather.8 = bf16[128,1024]{1,0:T(8,128)(2,1)S(1)} all-gather(bf16[8,1024]{1,0:T(8,128)(2,1)S(1)} %copy-done.6), channel_id=1, replica_groups=mesh['fsdp'=32,'cp'=16] {'cp'}, dimensions={0}, use_global_device_ids=true | all-gather | bytes 278528 | tf_op jit(solution)/shard_map/all_gather | solution.py:113
  138.0 1.2 broadcast_in_dim.53
  139.3 8.0 %all-to-all-start = ((bf16[128,32,128]{2,0,1:T(8,128)(2,1)}), bf16[128,32,128]{2,0,1:T(8,128)(2,1)S(1)}, u32[]{:S(2)}, u32[]{:S(2)}) async-start(bf16[128,32,128]{2,0,1:T(8,128)(2,1)} %bitcast.1), calls=%async_computation | async-start | bytes 2097152 | tf_op jit(solution)/shard_map/all_to_all | solution.py:120
  151.2 22.0 %all-to-all-done = bf16[128,32,128]{2,0,1:T(8,128)(2,1)S(1)} async-done(((bf16[128,32,128]{2,0,1:T(8,128)(2,1)}), bf16[128,32,128]{2,0,1:T(8,128)(2,1)S(1)}, u32[]{:S(2)}, u32[]{:S(2)}) %all-to-all-start) | async-done | bytes 1048608 | tf_op jit(solution)/shard_map/all_to_all | solution.py:120
  173.3 11.6 %while.30 = (s32[]{:T(128)}, f32[4,256]{1,0:T(4,128)S(1)}, f32[4,256]{1,0:T(4,128)S(1)}, f32[256,4,128]{0,2,1:T(8,128)S(1)}, s32[]{:T(128)}, /*index=5*/bf16[409...) while((s32[]{:T(128)}, f32[4,256]{1,0:T(4,128)S(1)}, ...), condition=%wide.region_3.4_spmd.clone, body=%wide.region_0.3_spmd.clone.sunk | while | flops 136909312 | bytes 4919495 | solution.py:46
  184.9 0.9 multiply_reduce_fusion
  186.5 1.5 broadcast.77
  187.9 57.6 %while.31 = (s32[]{:T(128)}, f32[256,4,128]{0,2,1:T(8,128)S(1)}, f32[4096,128]{1,0:T(8,128)}, f32[4096,128]{1,0:T(8,128)S(1)}, s32[]{:T(128)}, /*index=5*/bf16[4...) while((s32[]{:T(128)}, f32[256,4,128]{0,2,1:T(8,128)S(1)}, ...), condition=%wide.region_6.7_spmd.clone, body=%wide.region_5.6_spmd.clone.sunk | while | flops 337905152 | bytes 7680235 | solution.py:102
  188.1 1.2 fusion.94
  189.3 1.1 fusion.95
  190.4 1.1 fusion.96
  191.9 1.8 fusion.97
  193.8 1.2 fusion.94
  195.0 1.1 fusion.95
  196.2 1.1 fusion.96
  197.6 1.9 fusion.97
  199.6 1.2 fusion.94
  200.8 1.1 fusion.95
  202.0 1.1 fusion.96
  203.4 1.8 fusion.97
  205.3 1.2 fusion.94
  206.5 1.1 fusion.95
  207.7 1.1 fusion.96
  209.1 1.8 fusion.97
  211.1 1.2 fusion.94
  212.3 1.1 fusion.95
  213.5 1.1 fusion.96
  214.9 1.8 fusion.97
  216.8 1.2 fusion.94
  218.1 1.1 fusion.95
  219.2 1.1 fusion.96
  220.6 1.8 fusion.97
  222.6 1.2 fusion.94
  223.8 1.1 fusion.95
  225.0 1.1 fusion.96
  226.4 1.8 fusion.97
  228.3 1.2 fusion.94
  229.6 1.1 fusion.95
  230.7 1.1 fusion.96
  232.1 1.8 fusion.97
  234.1 1.2 fusion.94
  235.3 1.1 fusion.95
  236.5 1.1 fusion.96
  237.9 1.9 fusion.97
  239.9 1.2 fusion.94
  241.1 1.1 fusion.95
  242.2 1.1 fusion.96
  243.6 1.8 fusion.97
  245.5 1.1 convert_element_type.69
  246.6 6.0 all-to-all-start.3
  252.6 1.1 convert_element_type.63
  253.7 24.9 %all-to-all-done.3 = bf16[32,128,128]{2,1,0:T(8,128)(2,1)} async-done(((bf16[32,128,128]{2,1,0:T(8,128)(2,1)}), bf16[32,128,128]{2,1,0:T(8,128)(2,1)}, u32[]{:S(2)}, u32[]{:S(2)}) %all-to-all-start.3) | async-done | bytes 1048608 | tf_op jit(solution)/shard_map/all_to_all | solution.py:176
  278.6 5.8 all-to-all-start.2
  284.5 1.4 bitcast_reduce_fusion
  286.1 0.9 copy.85
  287.0 23.4 %all-to-all-done.2 = bf16[32,128,128]{2,1,0:T(8,128)(2,1)S(1)} async-done(((bf16[32,128,128]{2,1,0:T(8,128)(2,1)}), bf16[32,128,128]{2,1,0:T(8,128)(2,1)S(1)}, u32[]{:S(2)}, u32[]{:S(2)}) %all-to-all-start.2) | async-done | bytes 1048608 | tf_op jit(solution)/shard_map/all_to_all | solution.py:173
  310.7 0.8 copy.83
  313.3 227.3 %reduce-scatter.9.cloned.1.call-done = bf16[8,1024]{1,0:T(8,128)(2,1)} async-done(((bf16[128,1024]{1,0:T(8,128)(2,1)}), bf16[8,1024]{1,0:T(8,128)(2,1)}) %reduce-scatter.9.cloned.1.call-update) | async-done | bytes 16400
  540.5 0.9 copy.86
  542.2 218.4 %reduce-scatter.7.cloned.1.call-done = bf16[8,1024]{1,0:T(8,128)(2,1)} async-done(((bf16[128,1024]{1,0:T(8,128)(2,1)}), bf16[8,1024]{1,0:T(8,128)(2,1)}) %reduce-scatter.7.cloned.1.call-update) | async-done | bytes 16400
  760.6 0.9 copy.84
  (152 shorter events, 20.7 us)
Async XLA Ops:
  7.2 68.0 %copy-start.6 = (bf16[8,1024]{1,0:T(8,128)(2,1)S(1)}, bf16[8,1024]{1,0:T(8,128)(2,1)}, u32[]{:S(2)}) copy-start(bf16[8,1024]{1,0:T(8,128)(2,1)} %param.10) | copy-start | bytes 49156
  68.3 69.7 %all-to-all-start.1 = ((bf16[128,32,128]{2,0,1:T(8,128)(2,1)}), bf16[128,32,128]{2,0,1:T(8,128)(2,1)S(1)}, u32[]{:S(2)}, u32[]{:S(2)}) async-start(bf16[128,32,128]{2,0,1:T(8,128)(2,1)} %bitcast.6), calls=%async_computation.1 | async-start | bytes 2097152 | tf_op jit(solution)/shard_map/all_to_all | solution.py:121
  75.1 72.2 %copy-start.7 = (s32[32]{0:T(128)S(1)}, s32[32]{0:T(128)}, u32[]{:S(2)}) copy-start(s32[32]{0:T(128)} %param.13) | copy-start | bytes 388
  75.1 75.4 %copy-start.4 = (bf16[256,512]{1,0:T(8,128)(2,1)S(1)}, bf16[256,512]{1,0:T(8,128)(2,1)}, u32[]{:S(2)}) copy-start(bf16[256,512]{1,0:T(8,128)(2,1)} %param.12) | copy-start | bytes 786436
  138.0 12.8 %copy-start.5 = (bf16[256,512]{1,0:T(8,128)(2,1)S(1)}, bf16[256,512]{1,0:T(8,128)(2,1)}, u32[]{:S(2)}) copy-start(bf16[256,512]{1,0:T(8,128)(2,1)} %param.9) | copy-start | bytes 786436
  139.3 34.0 %all-to-all-start = ((bf16[128,32,128]{2,0,1:T(8,128)(2,1)}), bf16[128,32,128]{2,0,1:T(8,128)(2,1)S(1)}, u32[]{:S(2)}, u32[]{:S(2)}) async-start(bf16[128,32,128]{2,0,1:T(8,128)(2,1)} %bitcast.1), calls=%async_computation | async-start | bytes 2097152 | tf_op jit(solution)/shard_map/all_to_all | solution.py:120
  184.9 1.1 copy-start.1
  184.9 1.4 copy-start.2
  246.6 6.0 copy-start
  246.6 32.0 %all-to-all-start.3 = ((bf16[32,128,128]{2,1,0:T(8,128)(2,1)}), bf16[32,128,128]{2,1,0:T(8,128)(2,1)}, u32[]{:S(2)}, u32[]{:S(2)}) async-start(bf16[32,128,128]{2,1,0:T(8,128)(2,1)} %bitcast.152), calls=%async_computation.3 | async-start | bytes 2097152 | tf_op jit(solution)/shard_map/all_to_all | solution.py:176
  278.6 31.8 %all-to-all-start.2 = ((bf16[32,128,128]{2,1,0:T(8,128)(2,1)}), bf16[32,128,128]{2,1,0:T(8,128)(2,1)S(1)}, u32[]{:S(2)}, u32[]{:S(2)}) async-start(bf16[32,128,128]{2,1,0:T(8,128)(2,1)} %bitcast.151), calls=%async_computation.2 | async-start | bytes 2097152 | tf_op jit(solution)/shard_map/all_to_all | solution.py:173
  284.4 256.1 %reduce-scatter.9.cloned.1.call-start = ((), (), s32[]{:S(2)}) async-start(), calls=%async_computation.7 | async-start | bytes 278528
  285.9 25.7 %copy-start.3 = (bf16[256,4,128]{0,2,1:T(8,128)(2,1)S(1)}, bf16[256,4,128]{0,2,1:T(8,128)(2,1)}, u32[]{:S(2)}) copy-start(bf16[256,4,128]{0,2,1:T(8,128)(2,1)} %get-tuple-element.348) | copy-start | bytes 786436
  286.9 473.6 %reduce-scatter.7.cloned.1.call-start = ((), (), s32[]{:S(2)}) async-start(), calls=%async_computation.6 | async-start | bytes 278528
Sparse Core Ops, SparseCore 0:
  289.7 250.8 reduce-scatter.8
  545.0 215.5 reduce-scatter.6
where the time goes:
time: 772 us; the launch traced here: 769 us
  waiting for transfers between devices  516 us (67%)
  blocking collectives  123 us (16%)
  matrix products  63.5 us (8%)
  starting transfers between devices  26.8 us (3%)
  between operations  16.9 us (2%)
  local copies, waits for them, and re-layouts  12.9 us (2%)
  other arithmetic  9.22 us (1%)
    unnamed x4, waiting for transfers between devices  446 us
    all_gather x1, blocking collectives, fetch_keys(): lax.all_gather(key_vectors, 'cp', axis=0, tiled=True)  62.8 us
    all_gather x1, blocking collectives, fetch_keys(): lax.all_gather(value_vectors, 'cp', axis=0, tiled=True)  59.9 us
    all_to_all x1, waiting for transfers between devices, per_device(): lax.all_to_all(term_v.astype(jnp.bfloat16), 'fsdp', split_axis=0, concat_...  24.9 us
    all_to_all x1, waiting for transfers between devices, per_device(): lax.all_to_all(term_k.astype(jnp.bfloat16), 'fsdp', split_axis=0, concat_...  23.4 us
    all_to_all x1, waiting for transfers between devices, fetch_keys(): lax.all_to_all(spread_k, 'fsdp', split_axis=1, concat_axis=0, tiled=True)  22 us
    dot_general x10, matrix products, grad_step(): jnp.einsum('hnj,nhd->jd', score_grad, query_rows, preferred_element_type=...  18.5 us
    dot_general x20, matrix products, block_scores(): jnp.einsum('nhd,jd->hnj', query_rows, key_part, preferred_element_type=jn...  15.5 us
  transfers between devices with their start and end apart: 6, of which 5 were waited for; matrix products, arithmetic and copies ran while one was open for 1% of the time, Pallas kernels for 0%

commit v1 on v0

--- a/solution.py
+++ b/solution.py
@@ -6,6 +6,11 @@
 
 HD = 128
 NEG_FILL = -1e30
+
+
+def connect_the_targets(vector):
+    back = jnp.stack([vector for _ in range(lax.psum(1, axis_name="cp"))])
+    return jnp.concatenate(lax.all_to_all(back, "cp", split_axis=0, concat_axis=0), axis=0)
 
 
 def block_scores(query_rows, key_part, positions, key_start, score_scale):
@@ -110,7 +115,7 @@
     kv_heads = key_vectors.shape[1] // HD
     repeats = fsdp_size // kv_heads
     rows_k, rows_v = (
-        lax.all_gather(key_vectors, "cp", axis=0, tiled=True),
+        connect_the_targets(key_vectors),
         lax.all_gather(value_vectors, "cp", axis=0, tiled=True),
     )
     gathered_rows = rows_k.shape[0]

time: 772 us -> 749 us (0.970)
  blocking collectives: 123 us -> 55.4 us
  waiting for transfers between devices: 516 us -> 544 us
  starting transfers between devices: 26.8 us -> 40.9 us
    all_gather x1 -> x0, blocking collectives: 62.8 us -> none  [fetch_keys(): lax.all_gather(key_vectors, 'cp', axis=0, tiled=True)]
    all_to_all x1, waiting for transfers between devices: 0.01 us -> 25.8 us  [fetch_keys(): lax.all_to_all(spread_v, 'fsdp', split_axis=1, concat_axis=0, tiled=True)]
    all_to_all x0 -> x1, starting transfers between devices: none -> 15.6 us  [connect_the_targets(): lax.all_to_all(back, 'cp', split_axis=0, concat_axis=0)]
  transfers between devices with their start and end apart: 6 -> 7, of which waited for: 5 -> 6; matrix products, arithmetic and copies ran while one was open for 1% -> 1% of each run, Pallas kernels for 0% -> 0%
where the time goes in v1:
time: 749 us; the launch traced here: 746 us
  waiting for transfers between devices  544 us (73%)
  matrix products  63.6 us (8%)
  blocking collectives  55.4 us (7%)
  starting transfers between devices  40.9 us (5%)
  between operations  16.9 us (2%)
  local copies, waits for them, and re-layouts  14.4 us (2%)
  other arithmetic  9.22 us (1%)
    unnamed x4, waiting for transfers between devices  448 us
    all_gather x1, blocking collectives, fetch_keys(): lax.all_gather(value_vectors, 'cp', axis=0, tiled=True)  55.4 us
    all_to_all x1, waiting for transfers between devices, fetch_keys(): lax.all_to_all(spread_v, 'fsdp', split_axis=1, concat_axis=0, tiled=True)  25.8 us
    all_to_all x1, waiting for transfers between devices, per_device(): lax.all_to_all(term_v.astype(jnp.bfloat16), 'fsdp', split_axis=0, concat_...  24.9 us
    all_to_all x1, waiting for transfers between devices, per_device(): lax.all_to_all(term_k.astype(jnp.bfloat16), 'fsdp', split_axis=0, concat_...  23.4 us
    all_to_all x1, waiting for transfers between devices, fetch_keys(): lax.all_to_all(spread_k, 'fsdp', split_axis=1, concat_axis=0, tiled=True)  22 us
    dot_general x10, matrix products, grad_step(): jnp.einsum('hnj,nhd->jd', score_grad, query_rows, preferred_element_type=...  18.5 us
    all_to_all x1, starting transfers between devices, connect_the_targets(): lax.all_to_all(back, 'cp', split_axis=0, concat_axis=0)  15.6 us
  transfers between devices with their start and end apart: 7, of which 6 were waited for; matrix products, arithmetic and copies ran while one was open for 1% of the time, Pallas kernels for 0%

profile of v1, /device:TPU:4, one launch (start us, length us, event | category | flops | bytes accessed | tf_op | source)
XLA Modules:
  0.0 745.7 jit_solution(16475319339479097364)
XLA Ops:
  7.2 1.4 stack.2
  8.6 15.6 %all-to-all-start = ((bf16[16,8,1024]{2,1,0:T(8,128)(2,1)}), bf16[16,8,1024]{2,1,0:T(8,128)(2,1)S(1)}, u32[]{:S(2)}, u32[]{:S(2)}) async-start(bf16[16,8,1024]{2,1,0:T(8,128)(2,1)} %stack.2), calls=%async_computation | async-start | bytes 524288 | tf_op jit(solution)/shard_map/all_to_all | solution.py:13
  24.3 55.4 %all_gather.4 = bf16[128,1024]{1,0:T(8,128)(2,1)S(1)} all-gather(bf16[8,1024]{1,0:T(8,128)(2,1)} %param.11), channel_id=1, replica_groups=mesh['fsdp'=32,'cp'=16] {'cp'}, dimensions={0}, use_global_device_ids=true | all-gather | bytes 278528 | tf_op jit(solution)/shard_map/all_gather | solution.py:119
  79.7 1.2 broadcast_in_dim.54
  81.0 7.5 %all-to-all-start.2 = ((bf16[128,32,128]{2,0,1:T(8,128)(2,1)}), bf16[128,32,128]{2,0,1:T(8,128)(2,1)S(1)}, u32[]{:S(2)}, u32[]{:S(2)}) async-start(bf16[128,32,128]{2,0,1:T(8,128)(2,1)} %bitcast.6), calls=%async_computation.2 | async-start | bytes 2097152 | tf_op jit(solution)/shard_map/all_to_all | solution.py:126
  88.6 25.8 %all-to-all-done.2 = bf16[128,32,128]{2,0,1:T(8,128)(2,1)S(1)} async-done(((bf16[128,32,128]{2,0,1:T(8,128)(2,1)}), bf16[128,32,128]{2,0,1:T(8,128)(2,1)S(1)}, u32[]{:S(2)}, u32[]{:S(2)}) %all-to-all-start.2) | async-done | bytes 1048608 | tf_op jit(solution)/shard_map/all_to_all | solution.py:126
  114.4 1.2 broadcast_in_dim.53
  115.6 5.8 all-to-all-start.1
  125.3 22.0 %all-to-all-done.1 = bf16[128,32,128]{2,0,1:T(8,128)(2,1)S(1)} async-done(((bf16[128,32,128]{2,0,1:T(8,128)(2,1)}), bf16[128,32,128]{2,0,1:T(8,128)(2,1)S(1)}, u32[]{:S(2)}, u32[]{:S(2)}) %all-to-all-start.1) | async-done | bytes 1048608 | tf_op jit(solution)/shard_map/all_to_all | solution.py:125
  147.4 11.6 %while.30 = (s32[]{:T(128)}, f32[4,256]{1,0:T(4,128)S(1)}, f32[4,256]{1,0:T(4,128)S(1)}, f32[256,4,128]{0,2,1:T(8,128)S(1)}, s32[]{:T(128)}, /*index=5*/bf16[409...) while((s32[]{:T(128)}, f32[4,256]{1,0:T(4,128)S(1)}, ...), condition=%wide.region_3.4_spmd.clone, body=%wide.region_0.3_spmd.clone.sunk | while | flops 136909312 | bytes 4919495 | solution.py:51
  159.0 0.9 multiply_reduce_fusion
  160.6 1.5 broadcast.79
  162.1 57.6 %while.31 = (s32[]{:T(128)}, f32[256,4,128]{0,2,1:T(8,128)S(1)}, f32[4096,128]{1,0:T(8,128)}, f32[4096,128]{1,0:T(8,128)S(1)}, s32[]{:T(128)}, /*index=5*/bf16[4...) while((s32[]{:T(128)}, f32[256,4,128]{0,2,1:T(8,128)S(1)}, ...), condition=%wide.region_6.7_spmd.clone, body=%wide.region_5.6_spmd.clone.sunk | while | flops 337905152 | bytes 7680235 | solution.py:107
  162.2 1.2 fusion.93
  163.4 1.1 fusion.94
  164.6 1.1 fusion.95
  166.0 1.8 fusion.96
  167.9 1.2 fusion.93
  169.1 1.1 fusion.94
  170.3 1.1 fusion.95
  171.7 1.9 fusion.96
  173.7 1.2 fusion.93
  174.9 1.1 fusion.94
  176.1 1.1 fusion.95
  177.5 1.9 fusion.96
  179.5 1.2 fusion.93
  180.7 1.1 fusion.94
  181.8 1.1 fusion.95
  183.3 1.8 fusion.96
  185.2 1.2 fusion.93
  186.4 1.1 fusion.94
  187.6 1.1 fusion.95
  189.0 1.8 fusion.96
  191.0 1.2 fusion.93
  192.2 1.1 fusion.94
  193.3 1.1 fusion.95
  194.8 1.8 fusion.96
  196.7 1.2 fusion.93
  197.9 1.1 fusion.94
  199.1 1.1 fusion.95
  200.5 1.9 fusion.96
  202.5 1.2 fusion.93
  203.7 1.1 fusion.94
  204.9 1.1 fusion.95
  206.3 1.8 fusion.96
  208.2 1.2 fusion.93
  209.5 1.1 fusion.94
  210.6 1.1 fusion.95
  212.0 1.9 fusion.96
  214.0 1.2 fusion.93
  215.2 1.1 fusion.94
  216.4 1.1 fusion.95
  217.8 1.9 fusion.96
  219.7 1.1 convert_element_type.69
  220.8 6.0 all-to-all-start.4
  226.8 1.1 convert_element_type.63
  227.9 24.9 %all-to-all-done.4 = bf16[32,128,128]{2,1,0:T(8,128)(2,1)} async-done(((bf16[32,128,128]{2,1,0:T(8,128)(2,1)}), bf16[32,128,128]{2,1,0:T(8,128)(2,1)}, u32[]{:S(2)}, u32[]{:S(2)}) %all-to-all-start.4) | async-done | bytes 1048608 | tf_op jit(solution)/shard_map/all_to_all | solution.py:181
  252.7 5.8 all-to-all-start.3
  258.6 1.4 bitcast_reduce_fusion
  261.1 23.4 %all-to-all-done.3 = bf16[32,128,128]{2,1,0:T(8,128)(2,1)S(1)} async-done(((bf16[32,128,128]{2,1,0:T(8,128)(2,1)}), bf16[32,128,128]{2,1,0:T(8,128)(2,1)S(1)}, u32[]{:S(2)}, u32[]{:S(2)}) %all-to-all-start.3) | async-done | bytes 1048608 | tf_op jit(solution)/shard_map/all_to_all | solution.py:178
  287.5 229.8 %reduce-scatter.9.cloned.1.call-done = bf16[8,1024]{1,0:T(8,128)(2,1)} async-done(((bf16[128,1024]{1,0:T(8,128)(2,1)}), bf16[8,1024]{1,0:T(8,128)(2,1)}) %reduce-scatter.9.cloned.1.call-update) | async-done | bytes 16400
  517.2 0.9 copy.85
  518.9 218.4 %reduce-scatter.7.cloned.1.call-done = bf16[8,1024]{1,0:T(8,128)(2,1)} async-done(((bf16[128,1024]{1,0:T(8,128)(2,1)}), bf16[8,1024]{1,0:T(8,128)(2,1)}) %reduce-scatter.7.cloned.1.call-update) | async-done | bytes 16400
  737.3 0.9 copy.83
  (153 shorter events, 22.5 us)
Async XLA Ops:
  8.6 71.1 %all-to-all-start = ((bf16[16,8,1024]{2,1,0:T(8,128)(2,1)}), bf16[16,8,1024]{2,1,0:T(8,128)(2,1)S(1)}, u32[]{:S(2)}, u32[]{:S(2)}) async-start(bf16[16,8,1024]{2,1,0:T(8,128)(2,1)} %stack.2), calls=%async_computation | async-start | bytes 524288 | tf_op jit(solution)/shard_map/all_to_all | solution.py:13
  81.0 33.4 %all-to-all-start.2 = ((bf16[128,32,128]{2,0,1:T(8,128)(2,1)}), bf16[128,32,128]{2,0,1:T(8,128)(2,1)S(1)}, u32[]{:S(2)}, u32[]{:S(2)}) async-start(bf16[128,32,128]{2,0,1:T(8,128)(2,1)} %bitcast.6), calls=%async_computation.2 | async-start | bytes 2097152 | tf_op jit(solution)/shard_map/all_to_all | solution.py:126
  88.5 32.9 %copy-start.6 = (s32[32]{0:T(128)S(1)}, s32[32]{0:T(128)}, u32[]{:S(2)}) copy-start(s32[32]{0:T(128)} %param.13) | copy-start | bytes 388
  88.5 36.1 %copy-start.4 = (bf16[256,512]{1,0:T(8,128)(2,1)S(1)}, bf16[256,512]{1,0:T(8,128)(2,1)}, u32[]{:S(2)}) copy-start(bf16[256,512]{1,0:T(8,128)(2,1)} %param.12) | copy-start | bytes 786436
  88.6 36.4 %copy-start.5 = (bf16[256,512]{1,0:T(8,128)(2,1)S(1)}, bf16[256,512]{1,0:T(8,128)(2,1)}, u32[]{:S(2)}) copy-start(bf16[256,512]{1,0:T(8,128)(2,1)} %param.9) | copy-start | bytes 786436
  115.6 31.8 %all-to-all-start.1 = ((bf16[128,32,128]{2,0,1:T(8,128)(2,1)}), bf16[128,32,128]{2,0,1:T(8,128)(2,1)S(1)}, u32[]{:S(2)}, u32[]{:S(2)}) async-start(bf16[128,32,128]{2,0,1:T(8,128)(2,1)} %bitcast.1), calls=%async_computation.1 | async-start | bytes 2097152 | tf_op jit(solution)/shard_map/all_to_all | solution.py:125
  159.0 1.1 copy-start.1
  159.0 1.4 copy-start.2
  220.7 6.0 copy-start
  220.8 32.0 %all-to-all-start.4 = ((bf16[32,128,128]{2,1,0:T(8,128)(2,1)}), bf16[32,128,128]{2,1,0:T(8,128)(2,1)}, u32[]{:S(2)}, u32[]{:S(2)}) async-start(bf16[32,128,128]{2,1,0:T(8,128)(2,1)} %bitcast.150), calls=%async_computation.4 | async-start | bytes 2097152 | tf_op jit(solution)/shard_map/all_to_all | solution.py:181
  252.7 31.8 %all-to-all-start.3 = ((bf16[32,128,128]{2,1,0:T(8,128)(2,1)}), bf16[32,128,128]{2,1,0:T(8,128)(2,1)S(1)}, u32[]{:S(2)}, u32[]{:S(2)}) async-start(bf16[32,128,128]{2,1,0:T(8,128)(2,1)} %bitcast.149), calls=%async_computation.3 | async-start | bytes 2097152 | tf_op jit(solution)/shard_map/all_to_all | solution.py:178
  258.6 258.6 %reduce-scatter.9.cloned.1.call-start = ((), (), s32[]{:S(2)}) async-start(), calls=%async_computation.8 | async-start | bytes 278528
  260.0 25.7 %copy-start.3 = (bf16[256,4,128]{0,2,1:T(8,128)(2,1)S(1)}, bf16[256,4,128]{0,2,1:T(8,128)(2,1)}, u32[]{:S(2)}) copy-start(bf16[256,4,128]{0,2,1:T(8,128)(2,1)} %get-tuple-element.348) | copy-start | bytes 786436
  261.1 476.2 %reduce-scatter.7.cloned.1.call-start = ((), (), s32[]{:S(2)}) async-start(), calls=%async_computation.7 | async-start | bytes 278528
Sparse Core Ops, SparseCore 0:
  263.8 253.3 reduce-scatter.8
  521.7 215.5 reduce-scatter.6
